TPU v7x, 32 devices: a whole 2x2x4 slice. The times are simulated.
32 devices in a mesh: tile: 8 (over z, x), ka: 4 (over y, core).
Axes of the slice: x: 2, y: 2, z: 4, core: 2. Of those that a mesh axis runs over, the one named last changes fastest.
Arguments:
- amplitudes: bfloat16 [128, 32, 512], P(('tile', 'ka')), may hold values from -6 to 6
- integrals: bfloat16 [64, 512, 4096], P('tile', None, 'ka'), may hold values from -0.046875 to 0.046875
- slot_block: int32 [64], replicated, may hold values from 0 to 32, as said below
- rest: bfloat16 [128, 4096], P('tile', 'ka'), may hold values from -12 to 12
- occ_energy: float32 [128], P('tile'), may hold values from -2 to -0.5
- vir_energy: float32 [4096], P('ka'), may hold values from 0.5 to 3
Outputs:
- new_amp: bfloat16 [128, 4096], P('tile', 'ka')
Inputs may be any that keep to these rules, and one draw needn't show every extreme that they name: `slot_block`: each of the 32 blocks is stored in exactly one slot; the value 32 marks an empty slot. Slots s*8 to s*8 + 7 belong to owner s along tile; an owner holds 0 to 8 blocks, and some owner holds exactly 8.
All inputs are finite; a program needn't handle non-finite values.
Results may differ from a plain program's by a relative error of at most 0.001.
Values may be sent and summed in bfloat16 or wider, within the bound.
A program may use at most 128 MiB of HBM per device.

v0:
```python
import jax
import jax.numpy as jnp
from jax import lax
from jax.sharding import PartitionSpec as P


def per_device(amplitudes, integrals, slot_block, rest, occ_energy, vir_energy):
    capacity = integrals.shape[0]
    block_width = integrals.shape[1]
    tile_count = slot_block.shape[0] // capacity
    nblocks = amplitudes.shape[1]
    picker = (slot_block[:, None] == jnp.arange(nblocks, dtype=jnp.int32)[None, :]).astype(
        jnp.bfloat16
    )
    outgoing = jnp.einsum(
        "sg,rgb->srb", picker, amplitudes, preferred_element_type=jnp.float32
    ).astype(jnp.bfloat16)
    outgoing = outgoing.reshape(tile_count, capacity, amplitudes.shape[0], block_width)
    routed = lax.all_to_all(outgoing, "tile", split_axis=0, concat_axis=0, tiled=True)
    routed = routed[:, None]
    partial_value = jnp.einsum(
        "tksib,sbn->tkin",
        lax.all_gather(routed, "ka", axis=1, tiled=True),
        integrals,
        preferred_element_type=jnp.float32,
    )
    partial_value = partial_value.reshape(-1, partial_value.shape[-1])
    ladder = lax.psum_scatter(partial_value, "tile", scatter_dimension=0, tiled=True)
    denominator = vir_energy[None, :] - occ_energy[:, None]
    return ((rest.astype(jnp.float32) + ladder) / denominator).astype(jnp.bfloat16)


def solution(mesh):
    in_specs = (
        P(("tile", "ka"), None, None),
        P("tile", None, "ka"),
        P(),
        P("tile", "ka"),
        P("tile"),
        P("ka"),
    )
    out_specs = P("tile", "ka")
    return jax.shard_map(
        per_device, mesh=mesh, in_specs=in_specs, out_specs=out_specs, check_vma=False
    )
```

profile of v0, /device:TPU:0, one launch (start us, length us, event | category | flops | bytes accessed | tf_op | source)
XLA Modules:
  0.0 120.0 jit_solution(10600925300919967446)
XLA Ops:
  6.5 0.0 copy-start
  6.5 0.0 copy-start.2
  6.5 0.0 copy-start.3
  6.5 0.0 copy-start.1
  6.5 0.0 all-gather.3.cloned.1.call-start
  6.6 0.9 copy-done
  7.4 0.9 fusion.5
  8.4 16.1 %all_to_all.5 = bf16[8,8,4,512]{3,1,2,0:T(8,128)(2,1)} all-to-all(bf16[8,8,4,512]{3,1,2,0:T(8,128)(2,1)S(1)} %copy.7), channel_id=1, replica_groups=mesh['tile'=8,'ka'=4] {'tile'}, dimensions={0} | all-to-all | bytes 524288 | tf_op jit(solution)/shard_map/all_to_all | solution.py:19
  24.5 0.0 all-gather.3.cloned.1.call-update
  24.5 0.0 reduce-scatter.2.cloned.1.call-start
  24.6 15.8 %all-gather.3.cloned.1.call-done = bf16[8,32,4,512]{3,1,2,0:T(8,128)(2,1)} async-done(((bf16[8,8,4,512]{3,1,2,0:T(8,128)(2,1)}), bf16[8,32,4,512]{3,1,2,0:T(8,128)(2,1)}) %all-gather.3.cloned.1.call-update) | async-done | bytes 1048592 | tf_op jit(solution)/shard_map/all_gather | solution.py:23
  40.4 7.4 %fusion.2 = f32[8,4,4,1024]{3,2,1,0:T(4,128)S(1)} fusion(bf16[8,512,1024]{2,1,0:T(8,128)(2,1)} %param.7, bf16[8,4,8,4,512]{4,2,1,3,0:T(8,128)(2,1)} %bitcast.16), kind=kOutput, calls=%fused_computation.2 | convolution fusion | flops 1073741824 | bytes 9961472 | tf_op jit(solution)/shard_map/tksib,sbn->tkin/dot_general | solution.py:21
  47.9 1.0 reshape.10
  48.8 0.0 reduce-scatter.2.cloned.1.call-update
  48.9 62.8 %reduce-scatter.2.cloned.1.call-done = f32[16,1024]{1,0:T(8,128)} async-done(((f32[128,1024]{1,0:T(8,128)}), f32[16,1024]{1,0:T(8,128)}) %reduce-scatter.2.cloned.1.call-update) | async-done | bytes 65552 | tf_op jit(solution)/shard_map/reduce_scatter | solution.py:28
  111.6 0.0 copy-done.2
  111.6 0.0 copy-done.3
  111.6 0.0 copy-done.1
  111.6 1.5 %divide_convert_fusion = bf16[16,1024]{1,0:T(8,128)(2,1)} fusion(f32[16,1024]{1,0:T(8,128)} %reduce-scatter.2.cloned.1.call-done, bf16[16,1024]{1,0:T(8,128)(2,1)S(1)} %copy-done.1, f32[16]{0:T(128)S(1)} %copy-done.3, f32[1024]{0:T(1024)S(1)} %copy-done.2), kind=kLoop, calls=%fused_computation.6 | loop fusion | flops 81920 | bytes 135232 | tf_op jit(solution)/shard_map/convert_element_type | solution.py:30
  (1 shorter events, 0.0 us)
Async XLA Ops:
  6.5 0.9 copy-start
  6.5 105.1 %copy-start.2 = (f32[1024]{0:T(1024)S(1)}, f32[1024]{0:T(1024)}, u32[]{:S(2)}) copy-start(f32[1024]{0:T(1024)} %param.11) | copy-start | bytes 12292
  6.5 105.1 %copy-start.3 = (f32[16]{0:T(128)S(1)}, f32[16]{0:T(128)}, u32[]{:S(2)}) copy-start(f32[16]{0:T(128)} %param.10) | copy-start | bytes 196
  6.5 105.1 %copy-start.1 = (bf16[16,1024]{1,0:T(8,128)(2,1)S(1)}, bf16[16,1024]{1,0:T(8,128)(2,1)}, u32[]{:S(2)}) copy-start(bf16[16,1024]{1,0:T(8,128)(2,1)} %param.9) | copy-start | bytes 98308
  6.5 33.9 %all-gather.3.cloned.1.call-start = ((), (), s32[]{:S(2)}) async-start(), calls=%async_computation.3 | async-start | bytes 1310720 | tf_op jit(solution)/shard_map/all_gather | solution.py:23
  24.5 87.1 %reduce-scatter.2.cloned.1.call-start = ((), (), s32[]{:S(2)}) async-start(), calls=%async_computation.2 | async-start | bytes 589824 | tf_op jit(solution)/shard_map/reduce_scatter | solution.py:28
Sparse Core Ops, SparseCore 0:
  24.6 15.7 all-gather.2
  49.0 62.6 reduce-scatter.1
where the time goes:
time: 120 us
  waiting for transfers between devices  78.6 us (65%)
  blocking collectives  16.1 us (13%)
  between operations  13.4 us (11%)
  matrix products  8.37 us (7%)
  local copies, waits for them, and re-layouts  1.86 us (2%)
  other arithmetic  1.54 us (1%)
    reduce_scatter x1, waiting for transfers between devices, per_device(): lax.psum_scatter(partial_value, 'tile', scatter_dimension=0, tiled=True)  62.8 us
    all_to_all x1, blocking collectives, per_device(): lax.all_to_all(outgoing, 'tile', split_axis=0, concat_axis=0, tiled=True)  16.1 us
    all_gather x1, waiting for transfers between devices, per_device(): lax.all_gather(routed, 'ka', axis=1, tiled=True)  15.8 us
    dot_general x1, matrix products, per_device(): jnp.einsum('tksib,sbn->tkin', lax.all_gather(routed, 'ka', axis=1, tiled=...  7.44 us
  transfers between devices with their start and end apart: 2, of which 2 were waited for; matrix products, arithmetic and copies ran while one was open for 0% of the time, Pallas kernels for 0%

commit v1 on v0

--- a/solution.py
+++ b/solution.py
@@ -2,6 +2,30 @@
 import jax.numpy as jnp
 from jax import lax
 from jax.sharding import PartitionSpec as P
+
+
+def work_both_ways(x, axis, dim, work, out_dim):
+    size, index, extent = (lax.axis_size(axis), lax.axis_index(axis), x.shape[dim])
+    right = [(i, (i + 1) % size) for i in range(size)]
+    left = [(b, a) for a, b in right]
+    lower, upper = (lax.ppermute(x, axis, right), lax.ppermute(x, axis, left))
+    made = work(x, index * extent)
+    length = made.shape[out_dim]
+    out = jnp.zeros((*made.shape[:out_dim], size * length, *made.shape[out_dim + 1 :]), made.dtype)
+
+    def put(out, made, owner):
+        return lax.dynamic_update_slice_in_dim(out, made, owner * length, axis=out_dim)
+
+    out = put(out, made, index)
+    for lap in range(1, size // 2 + 1):
+        below, above = ((index - lap) % size, (index + lap) % size)
+        held = (lower, upper)
+        if lap < size // 2:
+            lower, upper = (lax.ppermute(lower, axis, right), lax.ppermute(upper, axis, left))
+        out = put(out, work(held[0], below * extent), below)
+        if 2 * lap < size:
+            out = put(out, work(held[1], above * extent), above)
+    return out
 
 
 def per_device(amplitudes, integrals, slot_block, rest, occ_energy, vir_energy):
@@ -18,11 +42,14 @@
     outgoing = outgoing.reshape(tile_count, capacity, amplitudes.shape[0], block_width)
     routed = lax.all_to_all(outgoing, "tile", split_axis=0, concat_axis=0, tiled=True)
     routed = routed[:, None]
-    partial_value = jnp.einsum(
-        "tksib,sbn->tkin",
-        lax.all_gather(routed, "ka", axis=1, tiled=True),
-        integrals,
-        preferred_element_type=jnp.float32,
+    partial_value = work_both_ways(
+        routed,
+        "ka",
+        1,
+        lambda part, offset: jnp.einsum(
+            "tksib,sbn->tkin", part, integrals, preferred_element_type=jnp.float32
+        ),
+        1,
     )
     partial_value = partial_value.reshape(-1, partial_value.shape[-1])
     ladder = lax.psum_scatter(partial_value, "tile", scatter_dimension=0, tiled=True)

time: 120 us -> 114 us (0.950)
  blocking collectives: 16.1 us -> 0 us
  starting transfers between devices: 0.08 us -> 7.88 us
  matrix products: 8.37 us -> 10.6 us
  waiting for transfers between devices: 78.6 us -> 77 us
  local copies, waits for them, and re-layouts: 1.86 us -> 3.3 us
    all_to_all x1 -> x0, blocking collectives: 16.1 us -> none  [per_device(): lax.all_to_all(outgoing, 'tile', split_axis=0, concat_axis=0, tiled=True)]
    all_gather x1 -> x0, waiting for transfers between devices: 15.8 us -> none  [per_device(): lax.all_gather(routed, 'ka', axis=1, tiled=True)]
    all_to_all x0 -> x1, waiting for transfers between devices: none -> 8.82 us  [per_device(): lax.all_to_all(outgoing, 'tile', split_axis=0, concat_axis=0, tiled=True)]
    all_to_all x0 -> x1, starting transfers between devices: none -> 7.28 us  [per_device(): lax.all_to_all(outgoing, 'tile', split_axis=0, concat_axis=0, tiled=True)]
    ppermute x0 -> x3, waiting for transfers between devices: none -> 6.78 us  [the longest x1 4.02 us: work_both_ways(): lax.ppermute(lower, axis, right)]
    dot_general x1 -> x4, matrix products: 7.44 us -> 9.69 us  [per_device(): jnp.einsum('tksib,sbn->tkin', part, integrals, preferred_element_type=jnp...]
    reduce_scatter x1, waiting for transfers between devices: 62.8 us -> 61.4 us  [per_device(): lax.psum_scatter(partial_value, 'tile', scatter_dimension=0, tiled=True)]
  transfers between devices with their start and end apart: 2 -> 5, of which waited for: 2 -> 4; matrix products, arithmetic and copies ran while one was open for 0% -> 8% of each run, Pallas kernels for 0% -> 0%
where the time goes in v1:
time: 114 us
  waiting for transfers between devices  77 us (68%)
  between operations  13.6 us (12%)
  matrix products  10.6 us (9%)
  starting transfers between devices  7.88 us (7%)
  local copies, waits for them, and re-layouts  3.3 us (3%)
  other arithmetic  1.54 us (1%)
    reduce_scatter x1, waiting for transfers between devices, per_device(): lax.psum_scatter(partial_value, 'tile', scatter_dimension=0, tiled=True)  61.4 us
    dot_general x4, matrix products, per_device(): jnp.einsum('tksib,sbn->tkin', part, integrals, preferred_element_type=jnp...  9.69 us
    all_to_all x1, waiting for transfers between devices, per_device(): lax.all_to_all(outgoing, 'tile', split_axis=0, concat_axis=0, tiled=True)  8.82 us
    all_to_all x1, starting transfers between devices, per_device(): lax.all_to_all(outgoing, 'tile', split_axis=0, concat_axis=0, tiled=True)  7.28 us
    ppermute x1, waiting for transfers between devices, work_both_ways(): lax.ppermute(lower, axis, right)  4.02 us
    ppermute x2, waiting for transfers between devices, work_both_ways(): lower, upper = (lax.ppermute(x, axis, right), lax.ppermute(x, axis, left))  2.75 us
  transfers between devices with their start and end apart: 5, of which 4 were waited for; matrix products, arithmetic and copies ran while one was open for 8% of the time, Pallas kernels for 0%

profile of v1, /device:TPU:0, one launch (start us, length us, event | category | flops | bytes accessed | tf_op | source)
XLA Modules:
  0.0 113.9 jit_solution(8255471606314252368)
XLA Ops:
  6.5 0.0 copy-start
  6.5 0.9 copy-done
  7.4 0.9 fusion.8
  8.4 0.7 copy.12
  9.1 7.3 %all-to-all-start = ((bf16[8,8,4,512]{3,1,2,0:T(8,128)(2,1)}), bf16[8,8,4,512]{3,1,2,0:T(8,128)(2,1)S(1)}, u32[]{:S(2)}, u32[]{:S(2)}) async-start(bf16[8,8,4,512]{3,1,2,0:T(8,128)(2,1)} %copy.12), calls=%async_computation | async-start | bytes 524288 | tf_op jit(solution)/shard_map/all_to_all | solution.py:43
  16.4 0.0 reduce-scatter.2.cloned.1.call-start
  16.5 8.8 %all-to-all-done = bf16[8,8,4,512]{3,1,2,0:T(8,128)(2,1)S(1)} async-done(((bf16[8,8,4,512]{3,1,2,0:T(8,128)(2,1)}), bf16[8,8,4,512]{3,1,2,0:T(8,128)(2,1)S(1)}, u32[]{:S(2)}, u32[]{:S(2)}) %all-to-all-start) | async-done | bytes 262176 | tf_op jit(solution)/shard_map/all_to_all | solution.py:43
  25.3 0.1 copy.30
  25.5 0.1 collective-permute-start.1
  25.5 0.5 collective-permute-start
  26.0 5.2 %fusion.9 = f32[8,1,4,1024]{3,0,2,1:T(8,128)S(1)} fusion(bf16[8,512,1024]{2,1,0:T(8,128)(2,1)} %param.7, bf16[8,8,4,512]{3,1,2,0:T(8,128)(2,1)S(1)} %all-to-all-done), kind=kOutput, calls=%fused_computation.10 | convolution fusion | flops 268435456 | bytes 8781824 | tf_op jit(solution)/shard_map/tksib,sbn->tkin/dot_general | solution.py:49
  31.2 0.1 broadcast_in_dim.4
  31.3 0.1 copy_dynamic-update-slice_fusion.3
  31.4 2.8 %collective-permute-done = bf16[8,1,8,4,512]{4,0,2,3,1:T(8,128)(2,1)S(1)} collective-permute-done((bf16[8,1,8,4,512]{4,0,2,3,1:T(8,128)(2,1)S(1)}, bf16[8,1,8,4,512]{4,0,2,3,1:T(8,128)(2,1)S(1)}, u32[]{:S(2)}, u32[]{:S(2)}) %collective-permute-start) | collective-permute-done | bytes 262176 | tf_op jit(solution)/shard_map/ppermute | solution.py:11
  34.2 0.0 copy-done.1
  34.2 1.5 %fusion.12 = f32[8,1,4,1024]{3,0,2,1:T(8,128)S(1)} fusion(bf16[8,512,1024]{2,1,0:T(8,128)(2,1)S(1)} %copy-done.1, bf16[8,1,8,4,512]{4,0,2,3,1:T(8,128)(2,1)S(1)} %collective-permute-done), kind=kOutput, calls=%fused_computation.11 | convolution fusion | flops 268435456 | bytes 8781824 | tf_op jit(solution)/shard_map/tksib,sbn->tkin/dot_general | solution.py:49
  35.7 0.0 collective-permute-start.2
  35.7 0.0 collective-permute-done.1
  35.7 1.5 %fusion.15 = f32[8,1,4,1024]{3,0,2,1:T(8,128)S(1)} fusion(bf16[8,512,1024]{2,1,0:T(8,128)(2,1)S(1)} %copy-done.1, bf16[8,1,8,4,512]{4,0,2,3,1:T(8,128)(2,1)S(1)} %collective-permute-done.1), kind=kOutput, calls=%fused_computation.12 | convolution fusion | flops 268435456 | bytes 8781824 | tf_op jit(solution)/shard_map/tksib,sbn->tkin/dot_general | solution.py:49
  37.2 0.0 copy-start.2
  37.2 0.0 copy-start.3
  37.2 0.0 copy-start.4
  37.3 0.1 copy_dynamic-update-slice_fusion.2
  37.4 0.1 copy_dynamic-update-slice_fusion.1
  37.5 4.0 %collective-permute-done.2 = bf16[8,1,8,4,512]{4,0,2,3,1:T(8,128)(2,1)S(1)} collective-permute-done((bf16[8,1,8,4,512]{4,0,2,3,1:T(8,128)(2,1)S(1)}, bf16[8,1,8,4,512]{4,0,2,3,1:T(8,128)(2,1)S(1)}, u32[]{:S(2)}, u32[]{:S(2)}) %collective-permute-start.2) | collective-permute-done | bytes 262176 | tf_op jit(solution)/shard_map/ppermute | solution.py:24
  41.5 1.5 %fusion.18 = f32[8,1,4,1024]{3,0,2,1:T(8,128)S(1)} fusion(bf16[8,512,1024]{2,1,0:T(8,128)(2,1)S(1)} %copy-done.1, bf16[8,1,8,4,512]{4,0,2,3,1:T(8,128)(2,1)S(1)} %collective-permute-done.2), kind=kOutput, calls=%fused_computation.13 | convolution fusion | flops 268435456 | bytes 8781824 | tf_op jit(solution)/shard_map/tksib,sbn->tkin/dot_general | solution.py:49
  43.0 0.1 copy_dynamic-update-slice_fusion
  43.1 1.0 reshape.28
  44.1 0.0 reduce-scatter.2.cloned.1.call-update
  44.1 61.4 %reduce-scatter.2.cloned.1.call-done = f32[16,1024]{1,0:T(8,128)} async-done(((f32[128,1024]{1,0:T(8,128)}), f32[16,1024]{1,0:T(8,128)}) %reduce-scatter.2.cloned.1.call-update) | async-done | bytes 65552 | tf_op jit(solution)/shard_map/reduce_scatter | solution.py:55
  105.5 0.0 copy-done.2
  105.5 1.5 %divide_convert_fusion = bf16[16,1024]{1,0:T(8,128)(2,1)} fusion(f32[16,1024]{1,0:T(8,128)} %reduce-scatter.2.cloned.1.call-done, bf16[16,1024]{1,0:T(8,128)(2,1)S(1)} %copy-done.2, f32[16]{0:T(128)S(1)} %copy-done.4, f32[1024]{0:T(1024)S(1)} %copy-done.3), kind=kLoop, calls=%fused_computation.23 | loop fusion | flops 81920 | bytes 135232 | tf_op jit(solution)/shard_map/convert_element_type | solution.py:57
  (3 shorter events, 0.0 us)
Async XLA Ops:
  6.5 0.9 copy-start
  9.1 16.2 %all-to-all-start = ((bf16[8,8,4,512]{3,1,2,0:T(8,128)(2,1)}), bf16[8,8,4,512]{3,1,2,0:T(8,128)(2,1)S(1)}, u32[]{:S(2)}, u32[]{:S(2)}) async-start(bf16[8,8,4,512]{3,1,2,0:T(8,128)(2,1)} %copy.12), calls=%async_computation | async-start | bytes 524288 | tf_op jit(solution)/shard_map/all_to_all | solution.py:43
  16.4 89.1 %reduce-scatter.2.cloned.1.call-start = ((), (), s32[]{:S(2)}) async-start(), calls=%async_computation.2 | async-start | bytes 589824 | tf_op jit(solution)/shard_map/reduce_scatter | solution.py:55
  25.3 8.9 %copy-start.1 = (bf16[8,512,1024]{2,1,0:T(8,128)(2,1)S(1)}, bf16[8,512,1024]{2,1,0:T(8,128)(2,1)}, u32[]{:S(2)}) copy-start(bf16[8,512,1024]{2,1,0:T(8,128)(2,1)} %param.7) | copy-start | bytes 25165828
  25.5 10.2 %collective-permute-start.1 = (bf16[8,1,8,4,512]{4,0,2,3,1:T(8,128)(2,1)S(1)}, bf16[8,1,8,4,512]{4,0,2,3,1:T(8,128)(2,1)S(1)}, u32[]{:S(2)}, u32[]{:S(2)}) collective-permute-start(bf16[8,1,8,4,512]{4,0,2,3,1:T(8,128)(2,1)S(1)} %bitcast.51), channel_id=1, source_target_pairs={{1,0},{2,1},{3,2},{0,3},{5,4},{6,5},{7,6},{4,7},{9,8},{10,9},{11,1... | collective-permute-start | bytes 786440 | tf_op jit(solution)/shard_map/ppermute | solution.py:11
  25.5 8.6 %collective-permute-start = (bf16[8,1,8,4,512]{4,0,2,3,1:T(8,128)(2,1)S(1)}, bf16[8,1,8,4,512]{4,0,2,3,1:T(8,128)(2,1)S(1)}, u32[]{:S(2)}, u32[]{:S(2)}) collective-permute-start(bf16[8,1,8,4,512]{4,0,2,3,1:T(8,128)(2,1)S(1)} %bitcast.52), channel_id=1, source_target_pairs={{0,1},{1,2},{2,3},{3,0},{4,5},{5,6},{6,7},{7,4},{8,9},{9,10},{10,1... | collective-permute-start | bytes 786440 | tf_op jit(solution)/shard_map/ppermute | solution.py:11
  35.7 5.8 %collective-permute-start.2 = (bf16[8,1,8,4,512]{4,0,2,3,1:T(8,128)(2,1)S(1)}, bf16[8,1,8,4,512]{4,0,2,3,1:T(8,128)(2,1)S(1)}, u32[]{:S(2)}, u32[]{:S(2)}) collective-permute-start(bf16[8,1,8,4,512]{4,0,2,3,1:T(8,128)(2,1)S(1)} %collective-permute-done), channel_id=1, source_target_pairs={{0,1},{1,2},{2,3},{3,0},{4,5},{5,6},{6,7},{7,4},{8,9},{9,10},{10,1... | collective-permute-start | bytes 786440 | tf_op jit(solution)/shard_map/ppermute | solution.py:24
  37.2 68.3 %copy-start.2 = (bf16[16,1024]{1,0:T(8,128)(2,1)S(1)}, bf16[16,1024]{1,0:T(8,128)(2,1)}, u32[]{:S(2)}) copy-start(bf16[16,1024]{1,0:T(8,128)(2,1)} %param.9) | copy-start | bytes 98308
  37.2 68.3 %copy-start.3 = (f32[1024]{0:T(1024)S(1)}, f32[1024]{0:T(1024)}, u32[]{:S(2)}) copy-start(f32[1024]{0:T(1024)} %param.11) | copy-start | bytes 12292
  37.2 68.3 %copy-start.4 = (f32[16]{0:T(128)S(1)}, f32[16]{0:T(128)}, u32[]{:S(2)}) copy-start(f32[16]{0:T(128)} %param.10) | copy-start | bytes 196
Sparse Core Ops, SparseCore 0:
  44.2 61.2 reduce-scatter.1
